TPU v7x, 256 devices: a whole 4x4x8 slice. The times are simulated.
256 devices in a mesh: seq: 32 (over y, z), head: 8 (over x, core).
Axes of the slice: x: 4, y: 4, z: 8, core: 2. Of those that a mesh axis runs over, the one named last changes fastest.
Arguments:
- query: bfloat16 [16384, 2048], P('seq', 'head'), may hold values from -6 to 6
- keys: bfloat16 [16384, 2048], P('seq', 'head'), may hold values from -6 to 6
- values: bfloat16 [16384, 4096], P('seq', 'head'), may hold values from -6 to 6
- gate_logit: float32 [16384, 32], P('seq', 'head'), may hold values from -17 to 1.5
- beta_logit: float32 [16384, 32], P('seq', 'head'), may hold values from -9 to 6
- decay_rate: float32 [32], P('head'), may hold values from 0.5 to 8
- norm_gain: float32 [128], replicated, may hold values from 0.1 to 1.9
- gate_z: bfloat16 [16384, 4096], P('seq', 'head'), may hold values from -6 to 6
- out_weight: bfloat16 [4096, 2048], P('head'), may hold values from -0.09375 to 0.09375
Outputs:
- mixed: bfloat16 [16384, 2048], P(('seq', 'head'))
All inputs are finite; a program needn't handle non-finite values.
Results may differ from a plain program's by a relative error of at most 0.014.
Values may be sent and summed in bfloat16 or wider, within the bound.
A program may use at most 128 MiB of HBM per device.

v0:
```python
import jax
import jax.numpy as jnp
from jax import lax
from jax.sharding import PartitionSpec as P

DK = 128
DV = 128
SPAN = 64


def passed_along(shard, axis, by):
    size = lax.axis_size(axis)
    pairs = [(i, i + by) for i in range(size) if 0 <= i + by < size]
    return lax.ppermute(shard, axis, pairs)


def unit_norm(values_in):
    return values_in * lax.rsqrt(jnp.sum(values_in * values_in, axis=-1, keepdims=True) + 1e-06)


def block_terms(query, keys, values, logdecay, beta):
    highest = lax.Precision.HIGHEST
    size = logdecay.shape[-1]
    width = keys.shape[-1]
    cumul = jnp.cumsum(logdecay, axis=-1)
    differ = cumul[..., :, None] - cumul[..., None, :]
    row_ids = lax.broadcasted_iota(jnp.int32, (size, size), 0)
    col_ids = lax.broadcasted_iota(jnp.int32, (size, size), 1)
    inclusive = col_ids <= row_ids
    strict = col_ids < row_ids
    ratio = jnp.where(inclusive, jnp.exp(jnp.where(inclusive, differ, 0.0)), 0.0)
    key_key = jnp.einsum("...te,...se->...ts", keys, keys, precision=highest)
    query_key = jnp.einsum("...te,...se->...ts", query, keys, precision=highest)
    lower = jnp.where(strict, beta[..., :, None] * ratio * key_key, 0.0) + jnp.eye(
        size, dtype=jnp.float32
    )
    rhs_values = beta[..., None] * values
    rhs_keys = (beta * jnp.exp(cumul))[..., None] * keys
    update = lax.linalg.triangular_solve(
        lower, rhs_values, left_side=True, lower=True, unit_diagonal=True
    )
    weights = lax.linalg.triangular_solve(
        lower, rhs_keys, left_side=True, lower=True, unit_diagonal=True
    )
    mixing = ratio * query_key
    decayed_query = jnp.exp(cumul)[..., None] * query
    key_end = jnp.exp(cumul[..., -1:] - cumul)[..., None] * keys
    transit = jnp.exp(cumul[..., -1])[..., None, None] * jnp.eye(width, dtype=jnp.float32)
    transit = transit - jnp.einsum("...se,...sf->...ef", key_end, weights, precision=highest)
    inject = jnp.einsum("...se,...sf->...ef", key_end, update, precision=highest)
    return (update, weights, mixing, decayed_query, transit, inject)


def run_blocks(terms, start):
    highest = lax.Precision.HIGHEST

    def advance(state, item):
        update, weights, mixing, decayed_query, transit, inject = item
        resid = update - jnp.einsum("...ce,...ef->...cf", weights, state, precision=highest)
        result = jnp.einsum("...ce,...ef->...cf", decayed_query, state, precision=highest)
        result = result + jnp.einsum("...ts,...sf->...tf", mixing, resid, precision=highest)
        state = jnp.einsum("...ef,...fg->...eg", transit, state, precision=highest) + inject
        return (state, result)

    return lax.scan(advance, start, terms)


def matmul_heads(left, right):
    return jnp.einsum("hef,hfg->heg", left, right, precision=lax.Precision.HIGHEST)


def on_device(
    query, keys, values, gate_logit, beta_logit, decay_rate, norm_gain, gate_z, out_weight
):
    tok_rows = query.shape[0]
    local_heads = values.shape[1] // DV
    key_heads = query.shape[1] // DK
    blocks = tok_rows // SPAN

    def to_blocks(array, width):
        return array.reshape(blocks, SPAN, local_heads, width).transpose(0, 2, 1, 3)

    qn = jnp.repeat(
        unit_norm(query.astype(jnp.float32).reshape(tok_rows, key_heads, DK)), 2, axis=1
    )
    kn = jnp.repeat(unit_norm(keys.astype(jnp.float32).reshape(tok_rows, key_heads, DK)), 2, axis=1)
    vals = values.astype(jnp.float32).reshape(tok_rows, local_heads, DV)
    logdecay = -decay_rate[None, :] * jax.nn.softplus(gate_logit)
    beta = jax.nn.sigmoid(beta_logit)
    terms = block_terms(
        to_blocks(qn, DK),
        to_blocks(kn, DK),
        to_blocks(vals, DV),
        logdecay.reshape(blocks, SPAN, local_heads).transpose(0, 2, 1),
        beta.reshape(blocks, SPAN, local_heads).transpose(0, 2, 1),
    )
    ident = jnp.broadcast_to(jnp.eye(DK, dtype=jnp.float32), (local_heads, DK, DK))
    zeros = jnp.zeros((local_heads, DK, DV), jnp.float32)

    def compose(carry, item):
        transit, inject = item
        return ((matmul_heads(transit, carry[0]), matmul_heads(transit, carry[1]) + inject), None)

    (shard_transit, shard_inject), unused = lax.scan(compose, (ident, zeros), (terms[4], terms[5]))

    def relay(step, carry):
        ending = matmul_heads(shard_transit, carry) + shard_inject
        return passed_along(ending, "seq", 1)

    start = lax.fori_loop(0, lax.axis_size("seq") - 1, relay, zeros)
    final, outs = run_blocks(terms, start)
    core = outs.transpose(0, 2, 1, 3).reshape(tok_rows, local_heads, DV)
    gate = jax.nn.silu(gate_z.astype(jnp.float32).reshape(tok_rows, local_heads, DV))
    scale = lax.rsqrt(jnp.mean(core * core, axis=-1, keepdims=True) + 1e-06)
    gated = (
        (core * scale * norm_gain * gate).astype(jnp.bfloat16).reshape(tok_rows, local_heads * DV)
    )
    rows = lax.all_to_all(gated, "head", split_axis=0, concat_axis=1, tiled=True)
    mixed = jnp.dot(
        rows,
        lax.all_gather(out_weight, "head", axis=0, tiled=True),
        preferred_element_type=jnp.float32,
    )
    return mixed.astype(jnp.bfloat16)


def solution(mesh):
    return jax.shard_map(
        on_device,
        mesh=mesh,
        in_specs=(
            P("seq", "head"),
            P("seq", "head"),
            P("seq", "head"),
            P("seq", "head"),
            P("seq", "head"),
            P("head"),
            P(),
            P("seq", "head"),
            P("head", None),
        ),
        out_specs=P(("seq", "head"), None),
        check_vma=False,
    )
```

profile of v0, /device:TPU:24, one launch (start us, length us, event | category | flops | bytes accessed | tf_op | source)
XLA Modules:
  0.0 647.6 jit_solution(6673752401664360787)
XLA Ops:
  12.7 2.0 fusion.30
  14.6 157.3 %custom-call.5 = f32[8,4,1,64,64]{3,4,2,1,0:T(8,128)S(1)} custom-call(f32[8,4,1,64,64]{4,3,2,1,0:T(8,128)S(1)} %fusion.30), custom_call_target="InvertDiagBlocksLowerTriangular" | custom-call | tf_op jit(solution)/shard_map/triangular_solve/custom-call.1 | solution.py:42
  178.4 2.1 fusion.36
  180.6 2.8 convolution_multiply_fusion
  183.4 4.8 fusion.44
  188.2 3.9 multiply_subtract_fusion
  192.2 14.6 %while.37 = (s32[]{:T(128)}, f32[4,128,128]{2,1,0:T(8,128)S(1)}, f32[4,128,128]{2,1,0:T(8,128)S(1)}, f32[8,4,128,128]{3,2,1,0:T(8,128)S(1)}, f32[8,4,128,128]{3,2,1,0:T(8,128)}, /*index=5*/s32[]{:T(128)}, s32[]{:T(128)}) while((s32[]{:T(128)}, f32[4,128,128]{2,1,0:T(8,128)S(1)}, f32[4,128,128]{2,1,0:T(8,128)S(1)}, ...), condition=%wide.region_3.5_spmd.clone, body=%wide.region_2.0_spmd.clone.sunk | while | flops 201457664 | bytes 2884699 | solution.py:104
  206.8 359.6 %while.35 = (s32[]{:T(128)}, f32[4,128,128]{2,1,0:T(8,128)S(1)}, f32[4,128,128]{2,1,0:T(8,128)S(1)}, f32[4,128,128]{2,1,0:T(8,128)S(1)}, s32[]{:T(128)}) while((s32[]{:T(128)}, f32[4,128,128]{2,1,0:T(8,128)S(1)}, f32[4,128,128]{2,1,0:T(8,128)S(1)}, f32[4,128,128]{2,1,0:T(8,128)S(1)}, s32[]{:T(128)}) %tuple.62), condition=%wide.region_5.7_spmd, body=%wide.region_4.6_spmd.sunk | while | flops 100728832 | bytes 2097253 | solution.py:110
  207.2 3.8 collective-permute-start
  211.1 10.4 %collective-permute-done = f32[4,128,128]{2,1,0:T(8,128)S(1)} collective-permute-done((f32[4,128,128]{2,1,0:T(8,128)S(1)}, f32[4,128,128]{2,1,0:T(8,128)S(1)}, u32[]{:S(2)}, u32[]{:S(2)}) %collective-permute-start) | collective-permute-done | bytes 262176 | tf_op jit(solution)/shard_map/while/body/eval_jaxpr/ppermute | solution.py:14
  223.8 9.6 %collective-permute-done = f32[4,128,128]{2,1,0:T(8,128)S(1)} collective-permute-done((f32[4,128,128]{2,1,0:T(8,128)S(1)}, f32[4,128,128]{2,1,0:T(8,128)S(1)}, u32[]{:S(2)}, u32[]{:S(2)}) %collective-permute-start) | collective-permute-done | bytes 262176 | tf_op jit(solution)/shard_map/while/body/eval_jaxpr/ppermute | solution.py:14
  235.7 8.6 %collective-permute-done = f32[4,128,128]{2,1,0:T(8,128)S(1)} collective-permute-done((f32[4,128,128]{2,1,0:T(8,128)S(1)}, f32[4,128,128]{2,1,0:T(8,128)S(1)}, u32[]{:S(2)}, u32[]{:S(2)}) %collective-permute-start) | collective-permute-done | bytes 262176 | tf_op jit(solution)/shard_map/while/body/eval_jaxpr/ppermute | solution.py:14
  246.7 8.4 %collective-permute-done = f32[4,128,128]{2,1,0:T(8,128)S(1)} collective-permute-done((f32[4,128,128]{2,1,0:T(8,128)S(1)}, f32[4,128,128]{2,1,0:T(8,128)S(1)}, u32[]{:S(2)}, u32[]{:S(2)}) %collective-permute-start) | collective-permute-done | bytes 262176 | tf_op jit(solution)/shard_map/while/body/eval_jaxpr/ppermute | solution.py:14
  257.5 8.4 %collective-permute-done = f32[4,128,128]{2,1,0:T(8,128)S(1)} collective-permute-done((f32[4,128,128]{2,1,0:T(8,128)S(1)}, f32[4,128,128]{2,1,0:T(8,128)S(1)}, u32[]{:S(2)}, u32[]{:S(2)}) %collective-permute-start) | collective-permute-done | bytes 262176 | tf_op jit(solution)/shard_map/while/body/eval_jaxpr/ppermute | solution.py:14
  268.2 8.4 %collective-permute-done = f32[4,128,128]{2,1,0:T(8,128)S(1)} collective-permute-done((f32[4,128,128]{2,1,0:T(8,128)S(1)}, f32[4,128,128]{2,1,0:T(8,128)S(1)}, u32[]{:S(2)}, u32[]{:S(2)}) %collective-permute-start) | collective-permute-done | bytes 262176 | tf_op jit(solution)/shard_map/while/body/eval_jaxpr/ppermute | solution.py:14
  279.0 8.5 %collective-permute-done = f32[4,128,128]{2,1,0:T(8,128)S(1)} collective-permute-done((f32[4,128,128]{2,1,0:T(8,128)S(1)}, f32[4,128,128]{2,1,0:T(8,128)S(1)}, u32[]{:S(2)}, u32[]{:S(2)}) %collective-permute-start) | collective-permute-done | bytes 262176 | tf_op jit(solution)/shard_map/while/body/eval_jaxpr/ppermute | solution.py:14
  289.9 9.6 %collective-permute-done = f32[4,128,128]{2,1,0:T(8,128)S(1)} collective-permute-done((f32[4,128,128]{2,1,0:T(8,128)S(1)}, f32[4,128,128]{2,1,0:T(8,128)S(1)}, u32[]{:S(2)}, u32[]{:S(2)}) %collective-permute-start) | collective-permute-done | bytes 262176 | tf_op jit(solution)/shard_map/while/body/eval_jaxpr/ppermute | solution.py:14
  301.8 10.8 %collective-permute-done = f32[4,128,128]{2,1,0:T(8,128)S(1)} collective-permute-done((f32[4,128,128]{2,1,0:T(8,128)S(1)}, f32[4,128,128]{2,1,0:T(8,128)S(1)}, u32[]{:S(2)}, u32[]{:S(2)}) %collective-permute-start) | collective-permute-done | bytes 262176 | tf_op jit(solution)/shard_map/while/body/eval_jaxpr/ppermute | solution.py:14
  315.0 10.5 %collective-permute-done = f32[4,128,128]{2,1,0:T(8,128)S(1)} collective-permute-done((f32[4,128,128]{2,1,0:T(8,128)S(1)}, f32[4,128,128]{2,1,0:T(8,128)S(1)}, u32[]{:S(2)}, u32[]{:S(2)}) %collective-permute-start) | collective-permute-done | bytes 262176 | tf_op jit(solution)/shard_map/while/body/eval_jaxpr/ppermute | solution.py:14
  327.9 9.7 %collective-permute-done = f32[4,128,128]{2,1,0:T(8,128)S(1)} collective-permute-done((f32[4,128,128]{2,1,0:T(8,128)S(1)}, f32[4,128,128]{2,1,0:T(8,128)S(1)}, u32[]{:S(2)}, u32[]{:S(2)}) %collective-permute-start) | collective-permute-done | bytes 262176 | tf_op jit(solution)/shard_map/while/body/eval_jaxpr/ppermute | solution.py:14
  339.9 8.8 %collective-permute-done = f32[4,128,128]{2,1,0:T(8,128)S(1)} collective-permute-done((f32[4,128,128]{2,1,0:T(8,128)S(1)}, f32[4,128,128]{2,1,0:T(8,128)S(1)}, u32[]{:S(2)}, u32[]{:S(2)}) %collective-permute-start) | collective-permute-done | bytes 262176 | tf_op jit(solution)/shard_map/while/body/eval_jaxpr/ppermute | solution.py:14
  351.0 8.4 %collective-permute-done = f32[4,128,128]{2,1,0:T(8,128)S(1)} collective-permute-done((f32[4,128,128]{2,1,0:T(8,128)S(1)}, f32[4,128,128]{2,1,0:T(8,128)S(1)}, u32[]{:S(2)}, u32[]{:S(2)}) %collective-permute-start) | collective-permute-done | bytes 262176 | tf_op jit(solution)/shard_map/while/body/eval_jaxpr/ppermute | solution.py:14
  361.8 8.4 %collective-permute-done = f32[4,128,128]{2,1,0:T(8,128)S(1)} collective-permute-done((f32[4,128,128]{2,1,0:T(8,128)S(1)}, f32[4,128,128]{2,1,0:T(8,128)S(1)}, u32[]{:S(2)}, u32[]{:S(2)}) %collective-permute-start) | collective-permute-done | bytes 262176 | tf_op jit(solution)/shard_map/while/body/eval_jaxpr/ppermute | solution.py:14
  372.6 8.4 %collective-permute-done = f32[4,128,128]{2,1,0:T(8,128)S(1)} collective-permute-done((f32[4,128,128]{2,1,0:T(8,128)S(1)}, f32[4,128,128]{2,1,0:T(8,128)S(1)}, u32[]{:S(2)}, u32[]{:S(2)}) %collective-permute-start) | collective-permute-done | bytes 262176 | tf_op jit(solution)/shard_map/while/body/eval_jaxpr/ppermute | solution.py:14
  383.4 8.4 %collective-permute-done = f32[4,128,128]{2,1,0:T(8,128)S(1)} collective-permute-done((f32[4,128,128]{2,1,0:T(8,128)S(1)}, f32[4,128,128]{2,1,0:T(8,128)S(1)}, u32[]{:S(2)}, u32[]{:S(2)}) %collective-permute-start) | collective-permute-done | bytes 262176 | tf_op jit(solution)/shard_map/while/body/eval_jaxpr/ppermute | solution.py:14
  394.2 9.5 %collective-permute-done = f32[4,128,128]{2,1,0:T(8,128)S(1)} collective-permute-done((f32[4,128,128]{2,1,0:T(8,128)S(1)}, f32[4,128,128]{2,1,0:T(8,128)S(1)}, u32[]{:S(2)}, u32[]{:S(2)}) %collective-permute-start) | collective-permute-done | bytes 262176 | tf_op jit(solution)/shard_map/while/body/eval_jaxpr/ppermute | solution.py:14
  406.0 10.7 %collective-permute-done = f32[4,128,128]{2,1,0:T(8,128)S(1)} collective-permute-done((f32[4,128,128]{2,1,0:T(8,128)S(1)}, f32[4,128,128]{2,1,0:T(8,128)S(1)}, u32[]{:S(2)}, u32[]{:S(2)}) %collective-permute-start) | collective-permute-done | bytes 262176 | tf_op jit(solution)/shard_map/while/body/eval_jaxpr/ppermute | solution.py:14
  419.1 10.6 %collective-permute-done = f32[4,128,128]{2,1,0:T(8,128)S(1)} collective-permute-done((f32[4,128,128]{2,1,0:T(8,128)S(1)}, f32[4,128,128]{2,1,0:T(8,128)S(1)}, u32[]{:S(2)}, u32[]{:S(2)}) %collective-permute-start) | collective-permute-done | bytes 262176 | tf_op jit(solution)/shard_map/while/body/eval_jaxpr/ppermute | solution.py:14
  432.1 9.8 %collective-permute-done = f32[4,128,128]{2,1,0:T(8,128)S(1)} collective-permute-done((f32[4,128,128]{2,1,0:T(8,128)S(1)}, f32[4,128,128]{2,1,0:T(8,128)S(1)}, u32[]{:S(2)}, u32[]{:S(2)}) %collective-permute-start) | collective-permute-done | bytes 262176 | tf_op jit(solution)/shard_map/while/body/eval_jaxpr/ppermute | solution.py:14
  444.2 8.9 %collective-permute-done = f32[4,128,128]{2,1,0:T(8,128)S(1)} collective-permute-done((f32[4,128,128]{2,1,0:T(8,128)S(1)}, f32[4,128,128]{2,1,0:T(8,128)S(1)}, u32[]{:S(2)}, u32[]{:S(2)}) %collective-permute-start) | collective-permute-done | bytes 262176 | tf_op jit(solution)/shard_map/while/body/eval_jaxpr/ppermute | solution.py:14
  455.5 8.4 %collective-permute-done = f32[4,128,128]{2,1,0:T(8,128)S(1)} collective-permute-done((f32[4,128,128]{2,1,0:T(8,128)S(1)}, f32[4,128,128]{2,1,0:T(8,128)S(1)}, u32[]{:S(2)}, u32[]{:S(2)}) %collective-permute-start) | collective-permute-done | bytes 262176 | tf_op jit(solution)/shard_map/while/body/eval_jaxpr/ppermute | solution.py:14
  466.2 8.4 %collective-permute-done = f32[4,128,128]{2,1,0:T(8,128)S(1)} collective-permute-done((f32[4,128,128]{2,1,0:T(8,128)S(1)}, f32[4,128,128]{2,1,0:T(8,128)S(1)}, u32[]{:S(2)}, u32[]{:S(2)}) %collective-permute-start) | collective-permute-done | bytes 262176 | tf_op jit(solution)/shard_map/while/body/eval_jaxpr/ppermute | solution.py:14
  477.0 8.4 %collective-permute-done = f32[4,128,128]{2,1,0:T(8,128)S(1)} collective-permute-done((f32[4,128,128]{2,1,0:T(8,128)S(1)}, f32[4,128,128]{2,1,0:T(8,128)S(1)}, u32[]{:S(2)}, u32[]{:S(2)}) %collective-permute-start) | collective-permute-done | bytes 262176 | tf_op jit(solution)/shard_map/while/body/eval_jaxpr/ppermute | solution.py:14
  487.8 8.4 %collective-permute-done = f32[4,128,128]{2,1,0:T(8,128)S(1)} collective-permute-done((f32[4,128,128]{2,1,0:T(8,128)S(1)}, f32[4,128,128]{2,1,0:T(8,128)S(1)}, u32[]{:S(2)}, u32[]{:S(2)}) %collective-permute-start) | collective-permute-done | bytes 262176 | tf_op jit(solution)/shard_map/while/body/eval_jaxpr/ppermute | solution.py:14
  498.6 9.4 %collective-permute-done = f32[4,128,128]{2,1,0:T(8,128)S(1)} collective-permute-done((f32[4,128,128]{2,1,0:T(8,128)S(1)}, f32[4,128,128]{2,1,0:T(8,128)S(1)}, u32[]{:S(2)}, u32[]{:S(2)}) %collective-permute-start) | collective-permute-done | bytes 262176 | tf_op jit(solution)/shard_map/while/body/eval_jaxpr/ppermute | solution.py:14
  510.3 10.6 %collective-permute-done = f32[4,128,128]{2,1,0:T(8,128)S(1)} collective-permute-done((f32[4,128,128]{2,1,0:T(8,128)S(1)}, f32[4,128,128]{2,1,0:T(8,128)S(1)}, u32[]{:S(2)}, u32[]{:S(2)}) %collective-permute-start) | collective-permute-done | bytes 262176 | tf_op jit(solution)/shard_map/while/body/eval_jaxpr/ppermute | solution.py:14
  523.3 10.7 %collective-permute-done = f32[4,128,128]{2,1,0:T(8,128)S(1)} collective-permute-done((f32[4,128,128]{2,1,0:T(8,128)S(1)}, f32[4,128,128]{2,1,0:T(8,128)S(1)}, u32[]{:S(2)}, u32[]{:S(2)}) %collective-permute-start) | collective-permute-done | bytes 262176 | tf_op jit(solution)/shard_map/while/body/eval_jaxpr/ppermute | solution.py:14
  536.4 8.4 %collective-permute-done = f32[4,128,128]{2,1,0:T(8,128)S(1)} collective-permute-done((f32[4,128,128]{2,1,0:T(8,128)S(1)}, f32[4,128,128]{2,1,0:T(8,128)S(1)}, u32[]{:S(2)}, u32[]{:S(2)}) %collective-permute-start) | collective-permute-done | bytes 262176 | tf_op jit(solution)/shard_map/while/body/eval_jaxpr/ppermute | solution.py:14
  547.2 8.4 %collective-permute-done = f32[4,128,128]{2,1,0:T(8,128)S(1)} collective-permute-done((f32[4,128,128]{2,1,0:T(8,128)S(1)}, f32[4,128,128]{2,1,0:T(8,128)S(1)}, u32[]{:S(2)}, u32[]{:S(2)}) %collective-permute-start) | collective-permute-done | bytes 262176 | tf_op jit(solution)/shard_map/while/body/eval_jaxpr/ppermute | solution.py:14
  557.9 8.4 %collective-permute-done = f32[4,128,128]{2,1,0:T(8,128)S(1)} collective-permute-done((f32[4,128,128]{2,1,0:T(8,128)S(1)}, f32[4,128,128]{2,1,0:T(8,128)S(1)}, u32[]{:S(2)}, u32[]{:S(2)}) %collective-permute-start) | collective-permute-done | bytes 262176 | tf_op jit(solution)/shard_map/while/body/eval_jaxpr/ppermute | solution.py:14
  566.4 46.7 %while.36 = (s32[]{:T(128)}, f32[4,128,128]{2,1,0:T(8,128)S(1)}, f32[8,4,64,128]{3,2,1,0:T(8,128)}, f32[8,4,128,128]{3,2,1,0:T(8,128)S(1)}, f32[8,4,128,128]{3,2...) while((s32[]{:T(128)}, f32[4,128,128]{2,1,0:T(8,128)S(1)}, ...), condition=%wide.region_8.10_spmd, body=%wide.region_7.9_spmd.sunk | while | flops 226623488 | bytes 3280485 | solution.py:65
  568.9 1.9 fusion.96
  580.6 1.9 fusion.96
  586.4 1.9 fusion.96
  604.0 1.9 fusion.96
  609.8 1.9 fusion.96
  616.7 14.5 %all_to_all.19 = bf16[8,64,512]{2,1,0:T(8,128)(2,1)S(1)} all-to-all(bf16[8,64,512]{2,1,0:T(8,128)(2,1)S(1)} %bitcast.135), channel_id=1, replica_groups=mesh['seq'=32,'head'=8] {'head'}, dimensions={0} | all-to-all | bytes 1048576 | tf_op jit(solution)/shard_map/all_to_all | solution.py:118
  631.2 9.5 %convolution_convert_fusion = bf16[64,2048]{1,0:T(8,128)(2,1)} fusion(bf16[64,4096]{1,0:T(8,128)(2,1)S(1)} %bitcast.133, bf16[4096,2048]{1,0:T(8,128)(2,1)} %all-gather.2.cloned.1.call-done), kind=kOutput, calls=%fused_computation.31 | convolution fusion | flops 1073872896 | bytes 17563648 | tf_op jit(solution)/shard_map/dot_general | solution.py:119
  (195 shorter events, 136.9 us)
Async XLA Ops:
  6.5 609.1 %copy-start = (f32[128]{0:T(128)S(1)}, f32[128]{0:T(128)}, u32[]{:S(2)}) copy-start(f32[128]{0:T(128)} %param.23) | copy-start | bytes 1540
  6.5 0.8 copy-start.9
  6.5 0.8 copy-start.7
  6.5 0.9 copy-start.8
  6.5 1.0 copy-start.5
  6.5 624.7 %all-gather.2.cloned.1.call-start = ((), (), s32[]{:S(2)}) async-start(), calls=%async_computation.1 | async-start | bytes 18874368 | tf_op jit(solution)/shard_map/all_gather | solution.py:121
  7.6 1.6 copy-start.6
  178.4 9.8 %copy-start.1 = (f32[8,4,64,128]{3,2,1,0:T(8,128)}, f32[8,4,64,128]{3,2,1,0:T(8,128)S(1)}, u32[]{:S(2)}) copy-start(f32[8,4,64,128]{3,2,1,0:T(8,128)S(1)} %fusion.38) | copy-start | bytes 3145732
  180.6 7.7 %copy-start.2 = (f32[8,4,64,128]{3,2,1,0:T(8,128)}, f32[8,4,64,128]{3,2,1,0:T(8,128)S(1)}, u32[]{:S(2)}) copy-start(f32[8,4,64,128]{3,2,1,0:T(8,128)S(1)} %fusion.36) | copy-start | bytes 3145732
  207.2 14.2 %collective-permute-start = (f32[4,128,128]{2,1,0:T(8,128)S(1)}, f32[4,128,128]{2,1,0:T(8,128)S(1)}, u32[]{:S(2)}, u32[]{:S(2)}) collective-permute-start(f32[4,128,128]{2,1,0:T(8,128)S(1)} %convolution_add_fusion.7), channel_id=1, source_target_pairs={{0,8},{8,16},{16,24},{24,32},{32,40},{40,48},{48,56},{56,64},{64,7... | collective-permute-start | bytes 786440 | tf_op jit(solution)/shard_map/while/body/eval_jaxpr/ppermute | solution.py:14
  221.9 11.5 %collective-permute-start = (f32[4,128,128]{2,1,0:T(8,128)S(1)}, f32[4,128,128]{2,1,0:T(8,128)S(1)}, u32[]{:S(2)}, u32[]{:S(2)}) collective-permute-start(f32[4,128,128]{2,1,0:T(8,128)S(1)} %convolution_add_fusion.7), channel_id=1, source_target_pairs={{0,8},{8,16},{16,24},{24,32},{32,40},{40,48},{48,56},{56,64},{64,7... | collective-permute-start | bytes 786440 | tf_op jit(solution)/shard_map/while/body/eval_jaxpr/ppermute | solution.py:14
  233.8 10.6 %collective-permute-start = (f32[4,128,128]{2,1,0:T(8,128)S(1)}, f32[4,128,128]{2,1,0:T(8,128)S(1)}, u32[]{:S(2)}, u32[]{:S(2)}) collective-permute-start(f32[4,128,128]{2,1,0:T(8,128)S(1)} %convolution_add_fusion.7), channel_id=1, source_target_pairs={{0,8},{8,16},{16,24},{24,32},{32,40},{40,48},{48,56},{56,64},{64,7... | collective-permute-start | bytes 786440 | tf_op jit(solution)/shard_map/while/body/eval_jaxpr/ppermute | solution.py:14
  244.8 10.4 %collective-permute-start = (f32[4,128,128]{2,1,0:T(8,128)S(1)}, f32[4,128,128]{2,1,0:T(8,128)S(1)}, u32[]{:S(2)}, u32[]{:S(2)}) collective-permute-start(f32[4,128,128]{2,1,0:T(8,128)S(1)} %convolution_add_fusion.7), channel_id=1, source_target_pairs={{0,8},{8,16},{16,24},{24,32},{32,40},{40,48},{48,56},{56,64},{64,7... | collective-permute-start | bytes 786440 | tf_op jit(solution)/shard_map/while/body/eval_jaxpr/ppermute | solution.py:14
  255.5 10.4 %collective-permute-start = (f32[4,128,128]{2,1,0:T(8,128)S(1)}, f32[4,128,128]{2,1,0:T(8,128)S(1)}, u32[]{:S(2)}, u32[]{:S(2)}) collective-permute-start(f32[4,128,128]{2,1,0:T(8,128)S(1)} %convolution_add_fusion.7), channel_id=1, source_target_pairs={{0,8},{8,16},{16,24},{24,32},{32,40},{40,48},{48,56},{56,64},{64,7... | collective-permute-start | bytes 786440 | tf_op jit(solution)/shard_map/while/body/eval_jaxpr/ppermute | solution.py:14
  266.3 10.4 %collective-permute-start = (f32[4,128,128]{2,1,0:T(8,128)S(1)}, f32[4,128,128]{2,1,0:T(8,128)S(1)}, u32[]{:S(2)}, u32[]{:S(2)}) collective-permute-start(f32[4,128,128]{2,1,0:T(8,128)S(1)} %convolution_add_fusion.7), channel_id=1, source_target_pairs={{0,8},{8,16},{16,24},{24,32},{32,40},{40,48},{48,56},{56,64},{64,7... | collective-permute-start | bytes 786440 | tf_op jit(solution)/shard_map/while/body/eval_jaxpr/ppermute | solution.py:14
  277.1 10.5 %collective-permute-start = (f32[4,128,128]{2,1,0:T(8,128)S(1)}, f32[4,128,128]{2,1,0:T(8,128)S(1)}, u32[]{:S(2)}, u32[]{:S(2)}) collective-permute-start(f32[4,128,128]{2,1,0:T(8,128)S(1)} %convolution_add_fusion.7), channel_id=1, source_target_pairs={{0,8},{8,16},{16,24},{24,32},{32,40},{40,48},{48,56},{56,64},{64,7... | collective-permute-start | bytes 786440 | tf_op jit(solution)/shard_map/while/body/eval_jaxpr/ppermute | solution.py:14
  288.0 11.5 %collective-permute-start = (f32[4,128,128]{2,1,0:T(8,128)S(1)}, f32[4,128,128]{2,1,0:T(8,128)S(1)}, u32[]{:S(2)}, u32[]{:S(2)}) collective-permute-start(f32[4,128,128]{2,1,0:T(8,128)S(1)} %convolution_add_fusion.7), channel_id=1, source_target_pairs={{0,8},{8,16},{16,24},{24,32},{32,40},{40,48},{48,56},{56,64},{64,7... | collective-permute-start | bytes 786440 | tf_op jit(solution)/shard_map/while/body/eval_jaxpr/ppermute | solution.py:14
  299.9 12.8 %collective-permute-start = (f32[4,128,128]{2,1,0:T(8,128)S(1)}, f32[4,128,128]{2,1,0:T(8,128)S(1)}, u32[]{:S(2)}, u32[]{:S(2)}) collective-permute-start(f32[4,128,128]{2,1,0:T(8,128)S(1)} %convolution_add_fusion.7), channel_id=1, source_target_pairs={{0,8},{8,16},{16,24},{24,32},{32,40},{40,48},{48,56},{56,64},{64,7... | collective-permute-start | bytes 786440 | tf_op jit(solution)/shard_map/while/body/eval_jaxpr/ppermute | solution.py:14
  313.1 12.5 %collective-permute-start = (f32[4,128,128]{2,1,0:T(8,128)S(1)}, f32[4,128,128]{2,1,0:T(8,128)S(1)}, u32[]{:S(2)}, u32[]{:S(2)}) collective-permute-start(f32[4,128,128]{2,1,0:T(8,128)S(1)} %convolution_add_fusion.7), channel_id=1, source_target_pairs={{0,8},{8,16},{16,24},{24,32},{32,40},{40,48},{48,56},{56,64},{64,7... | collective-permute-start | bytes 786440 | tf_op jit(solution)/shard_map/while/body/eval_jaxpr/ppermute | solution.py:14
  325.9 11.6 %collective-permute-start = (f32[4,128,128]{2,1,0:T(8,128)S(1)}, f32[4,128,128]{2,1,0:T(8,128)S(1)}, u32[]{:S(2)}, u32[]{:S(2)}) collective-permute-start(f32[4,128,128]{2,1,0:T(8,128)S(1)} %convolution_add_fusion.7), channel_id=1, source_target_pairs={{0,8},{8,16},{16,24},{24,32},{32,40},{40,48},{48,56},{56,64},{64,7... | collective-permute-start | bytes 786440 | tf_op jit(solution)/shard_map/while/body/eval_jaxpr/ppermute | solution.py:14
  338.0 10.7 %collective-permute-start = (f32[4,128,128]{2,1,0:T(8,128)S(1)}, f32[4,128,128]{2,1,0:T(8,128)S(1)}, u32[]{:S(2)}, u32[]{:S(2)}) collective-permute-start(f32[4,128,128]{2,1,0:T(8,128)S(1)} %convolution_add_fusion.7), channel_id=1, source_target_pairs={{0,8},{8,16},{16,24},{24,32},{32,40},{40,48},{48,56},{56,64},{64,7... | collective-permute-start | bytes 786440 | tf_op jit(solution)/shard_map/while/body/eval_jaxpr/ppermute | solution.py:14
  349.1 10.4 %collective-permute-start = (f32[4,128,128]{2,1,0:T(8,128)S(1)}, f32[4,128,128]{2,1,0:T(8,128)S(1)}, u32[]{:S(2)}, u32[]{:S(2)}) collective-permute-start(f32[4,128,128]{2,1,0:T(8,128)S(1)} %convolution_add_fusion.7), channel_id=1, source_target_pairs={{0,8},{8,16},{16,24},{24,32},{32,40},{40,48},{48,56},{56,64},{64,7... | collective-permute-start | bytes 786440 | tf_op jit(solution)/shard_map/while/body/eval_jaxpr/ppermute | solution.py:14
  359.9 10.4 %collective-permute-start = (f32[4,128,128]{2,1,0:T(8,128)S(1)}, f32[4,128,128]{2,1,0:T(8,128)S(1)}, u32[]{:S(2)}, u32[]{:S(2)}) collective-permute-start(f32[4,128,128]{2,1,0:T(8,128)S(1)} %convolution_add_fusion.7), channel_id=1, source_target_pairs={{0,8},{8,16},{16,24},{24,32},{32,40},{40,48},{48,56},{56,64},{64,7... | collective-permute-start | bytes 786440 | tf_op jit(solution)/shard_map/while/body/eval_jaxpr/ppermute | solution.py:14
  370.7 10.4 %collective-permute-start = (f32[4,128,128]{2,1,0:T(8,128)S(1)}, f32[4,128,128]{2,1,0:T(8,128)S(1)}, u32[]{:S(2)}, u32[]{:S(2)}) collective-permute-start(f32[4,128,128]{2,1,0:T(8,128)S(1)} %convolution_add_fusion.7), channel_id=1, source_target_pairs={{0,8},{8,16},{16,24},{24,32},{32,40},{40,48},{48,56},{56,64},{64,7... | collective-permute-start | bytes 786440 | tf_op jit(solution)/shard_map/while/body/eval_jaxpr/ppermute | solution.py:14
  381.5 10.4 %collective-permute-start = (f32[4,128,128]{2,1,0:T(8,128)S(1)}, f32[4,128,128]{2,1,0:T(8,128)S(1)}, u32[]{:S(2)}, u32[]{:S(2)}) collective-permute-start(f32[4,128,128]{2,1,0:T(8,128)S(1)} %convolution_add_fusion.7), channel_id=1, source_target_pairs={{0,8},{8,16},{16,24},{24,32},{32,40},{40,48},{48,56},{56,64},{64,7... | collective-permute-start | bytes 786440 | tf_op jit(solution)/shard_map/while/body/eval_jaxpr/ppermute | solution.py:14
  392.2 11.5 %collective-permute-start = (f32[4,128,128]{2,1,0:T(8,128)S(1)}, f32[4,128,128]{2,1,0:T(8,128)S(1)}, u32[]{:S(2)}, u32[]{:S(2)}) collective-permute-start(f32[4,128,128]{2,1,0:T(8,128)S(1)} %convolution_add_fusion.7), channel_id=1, source_target_pairs={{0,8},{8,16},{16,24},{24,32},{32,40},{40,48},{48,56},{56,64},{64,7... | collective-permute-start | bytes 786440 | tf_op jit(solution)/shard_map/while/body/eval_jaxpr/ppermute | solution.py:14
  404.1 12.7 %collective-permute-start = (f32[4,128,128]{2,1,0:T(8,128)S(1)}, f32[4,128,128]{2,1,0:T(8,128)S(1)}, u32[]{:S(2)}, u32[]{:S(2)}) collective-permute-start(f32[4,128,128]{2,1,0:T(8,128)S(1)} %convolution_add_fusion.7), channel_id=1, source_target_pairs={{0,8},{8,16},{16,24},{24,32},{32,40},{40,48},{48,56},{56,64},{64,7... | collective-permute-start | bytes 786440 | tf_op jit(solution)/shard_map/while/body/eval_jaxpr/ppermute | solution.py:14
  417.2 12.6 %collective-permute-start = (f32[4,128,128]{2,1,0:T(8,128)S(1)}, f32[4,128,128]{2,1,0:T(8,128)S(1)}, u32[]{:S(2)}, u32[]{:S(2)}) collective-permute-start(f32[4,128,128]{2,1,0:T(8,128)S(1)} %convolution_add_fusion.7), channel_id=1, source_target_pairs={{0,8},{8,16},{16,24},{24,32},{32,40},{40,48},{48,56},{56,64},{64,7... | collective-permute-start | bytes 786440 | tf_op jit(solution)/shard_map/while/body/eval_jaxpr/ppermute | solution.py:14
  430.1 11.8 %collective-permute-start = (f32[4,128,128]{2,1,0:T(8,128)S(1)}, f32[4,128,128]{2,1,0:T(8,128)S(1)}, u32[]{:S(2)}, u32[]{:S(2)}) collective-permute-start(f32[4,128,128]{2,1,0:T(8,128)S(1)} %convolution_add_fusion.7), channel_id=1, source_target_pairs={{0,8},{8,16},{16,24},{24,32},{32,40},{40,48},{48,56},{56,64},{64,7... | collective-permute-start | bytes 786440 | tf_op jit(solution)/shard_map/while/body/eval_jaxpr/ppermute | solution.py:14
  442.3 10.8 %collective-permute-start = (f32[4,128,128]{2,1,0:T(8,128)S(1)}, f32[4,128,128]{2,1,0:T(8,128)S(1)}, u32[]{:S(2)}, u32[]{:S(2)}) collective-permute-start(f32[4,128,128]{2,1,0:T(8,128)S(1)} %convolution_add_fusion.7), channel_id=1, source_target_pairs={{0,8},{8,16},{16,24},{24,32},{32,40},{40,48},{48,56},{56,64},{64,7... | collective-permute-start | bytes 786440 | tf_op jit(solution)/shard_map/while/body/eval_jaxpr/ppermute | solution.py:14
  453.5 10.4 %collective-permute-start = (f32[4,128,128]{2,1,0:T(8,128)S(1)}, f32[4,128,128]{2,1,0:T(8,128)S(1)}, u32[]{:S(2)}, u32[]{:S(2)}) collective-permute-start(f32[4,128,128]{2,1,0:T(8,128)S(1)} %convolution_add_fusion.7), channel_id=1, source_target_pairs={{0,8},{8,16},{16,24},{24,32},{32,40},{40,48},{48,56},{56,64},{64,7... | collective-permute-start | bytes 786440 | tf_op jit(solution)/shard_map/while/body/eval_jaxpr/ppermute | solution.py:14
  464.3 10.4 %collective-permute-start = (f32[4,128,128]{2,1,0:T(8,128)S(1)}, f32[4,128,128]{2,1,0:T(8,128)S(1)}, u32[]{:S(2)}, u32[]{:S(2)}) collective-permute-start(f32[4,128,128]{2,1,0:T(8,128)S(1)} %convolution_add_fusion.7), channel_id=1, source_target_pairs={{0,8},{8,16},{16,24},{24,32},{32,40},{40,48},{48,56},{56,64},{64,7... | collective-permute-start | bytes 786440 | tf_op jit(solution)/shard_map/while/body/eval_jaxpr/ppermute | solution.py:14
  475.1 10.4 %collective-permute-start = (f32[4,128,128]{2,1,0:T(8,128)S(1)}, f32[4,128,128]{2,1,0:T(8,128)S(1)}, u32[]{:S(2)}, u32[]{:S(2)}) collective-permute-start(f32[4,128,128]{2,1,0:T(8,128)S(1)} %convolution_add_fusion.7), channel_id=1, source_target_pairs={{0,8},{8,16},{16,24},{24,32},{32,40},{40,48},{48,56},{56,64},{64,7... | collective-permute-start | bytes 786440 | tf_op jit(solution)/shard_map/while/body/eval_jaxpr/ppermute | solution.py:14
  485.9 10.4 %collective-permute-start = (f32[4,128,128]{2,1,0:T(8,128)S(1)}, f32[4,128,128]{2,1,0:T(8,128)S(1)}, u32[]{:S(2)}, u32[]{:S(2)}) collective-permute-start(f32[4,128,128]{2,1,0:T(8,128)S(1)} %convolution_add_fusion.7), channel_id=1, source_target_pairs={{0,8},{8,16},{16,24},{24,32},{32,40},{40,48},{48,56},{56,64},{64,7... | collective-permute-start | bytes 786440 | tf_op jit(solution)/shard_map/while/body/eval_jaxpr/ppermute | solution.py:14
  496.7 11.4 %collective-permute-start = (f32[4,128,128]{2,1,0:T(8,128)S(1)}, f32[4,128,128]{2,1,0:T(8,128)S(1)}, u32[]{:S(2)}, u32[]{:S(2)}) collective-permute-start(f32[4,128,128]{2,1,0:T(8,128)S(1)} %convolution_add_fusion.7), channel_id=1, source_target_pairs={{0,8},{8,16},{16,24},{24,32},{32,40},{40,48},{48,56},{56,64},{64,7... | collective-permute-start | bytes 786440 | tf_op jit(solution)/shard_map/while/body/eval_jaxpr/ppermute | solution.py:14
  508.4 12.5 %collective-permute-start = (f32[4,128,128]{2,1,0:T(8,128)S(1)}, f32[4,128,128]{2,1,0:T(8,128)S(1)}, u32[]{:S(2)}, u32[]{:S(2)}) collective-permute-start(f32[4,128,128]{2,1,0:T(8,128)S(1)} %convolution_add_fusion.7), channel_id=1, source_target_pairs={{0,8},{8,16},{16,24},{24,32},{32,40},{40,48},{48,56},{56,64},{64,7... | collective-permute-start | bytes 786440 | tf_op jit(solution)/shard_map/while/body/eval_jaxpr/ppermute | solution.py:14
  521.4 12.7 %collective-permute-start = (f32[4,128,128]{2,1,0:T(8,128)S(1)}, f32[4,128,128]{2,1,0:T(8,128)S(1)}, u32[]{:S(2)}, u32[]{:S(2)}) collective-permute-start(f32[4,128,128]{2,1,0:T(8,128)S(1)} %convolution_add_fusion.7), channel_id=1, source_target_pairs={{0,8},{8,16},{16,24},{24,32},{32,40},{40,48},{48,56},{56,64},{64,7... | collective-permute-start | bytes 786440 | tf_op jit(solution)/shard_map/while/body/eval_jaxpr/ppermute | solution.py:14
  534.4 10.4 %collective-permute-start = (f32[4,128,128]{2,1,0:T(8,128)S(1)}, f32[4,128,128]{2,1,0:T(8,128)S(1)}, u32[]{:S(2)}, u32[]{:S(2)}) collective-permute-start(f32[4,128,128]{2,1,0:T(8,128)S(1)} %convolution_add_fusion.7), channel_id=1, source_target_pairs={{0,8},{8,16},{16,24},{24,32},{32,40},{40,48},{48,56},{56,64},{64,7... | collective-permute-start | bytes 786440 | tf_op jit(solution)/shard_map/while/body/eval_jaxpr/ppermute | solution.py:14
  545.2 10.4 %collective-permute-start = (f32[4,128,128]{2,1,0:T(8,128)S(1)}, f32[4,128,128]{2,1,0:T(8,128)S(1)}, u32[]{:S(2)}, u32[]{:S(2)}) collective-permute-start(f32[4,128,128]{2,1,0:T(8,128)S(1)} %convolution_add_fusion.7), channel_id=1, source_target_pairs={{0,8},{8,16},{16,24},{24,32},{32,40},{40,48},{48,56},{56,64},{64,7... | collective-permute-start | bytes 786440 | tf_op jit(solution)/shard_map/while/body/eval_jaxpr/ppermute | solution.py:14
  556.0 10.4 %collective-permute-start = (f32[4,128,128]{2,1,0:T(8,128)S(1)}, f32[4,128,128]{2,1,0:T(8,128)S(1)}, u32[]{:S(2)}, u32[]{:S(2)}) collective-permute-start(f32[4,128,128]{2,1,0:T(8,128)S(1)} %convolution_add_fusion.7), channel_id=1, source_target_pairs={{0,8},{8,16},{16,24},{24,32},{32,40},{40,48},{48,56},{56,64},{64,7... | collective-permute-start | bytes 786440 | tf_op jit(solution)/shard_map/while/body/eval_jaxpr/ppermute | solution.py:14
  613.1 1.9 copy-start.3
  614.8 1.5 copy-start.4
Sparse Core Ops, SparseCore 0:
  9.2 90.7 all-gather.1
where the time goes:
time: 650 us; the launch traced here: 648 us
  waiting for transfers between devices  286 us (44%)
  other arithmetic  165 us (25%)
  matrix products  99.5 us (15%)
  starting transfers between devices  61.5 us (9%)
  blocking collectives  14.5 us (2%)
  between operations  13.7 us (2%)
    ppermute x31, waiting for transfers between devices, passed_along(): return lax.ppermute(shard, axis, pairs)  285 us
    another operation x4, other arithmetic, block_terms(): lax.linalg.triangular_solve(lower, rhs_keys, left_side=True, lower=True,...  157 us
    ppermute x31, starting transfers between devices, passed_along(): return lax.ppermute(shard, axis, pairs)  61.4 us
    dot_general x47, matrix products, matmul_heads(): jnp.einsum('hef,hfg->heg', left, right, precision=lax.Precision.HIGHEST)  26.2 us
    dot_general x8, matrix products, advance(): jnp.einsum('...ce,...ef->...cf', decayed_query, state, precision=highest)  15.5 us
    all_to_all x1, blocking collectives, on_device(): lax.all_to_all(gated, 'head', split_axis=0, concat_axis=1, tiled=True)  14.5 us
  transfers between devices with their start and end apart: 32, of which 31 were waited for; matrix products, arithmetic and copies ran while one was open for 40% of the time, Pallas kernels for 0%

commit v1 on v0

--- a/solution.py
+++ b/solution.py
@@ -115,7 +115,9 @@
     gated = (
         (core * scale * norm_gain * gate).astype(jnp.bfloat16).reshape(tok_rows, local_heads * DV)
     )
-    rows = lax.all_to_all(gated, "head", split_axis=0, concat_axis=1, tiled=True)
+    shards = jnp.split(gated, lax.axis_size("head"), axis=0)
+    got = lax.all_to_all(jnp.stack(shards), "head", 0, 0)
+    rows = jnp.concatenate(got, axis=1)
     mixed = jnp.dot(
         rows,
         lax.all_gather(out_weight, "head", axis=0, tiled=True),

time: 650 us -> 649 us (level)
  no operation moved by 1% of the time
where the time goes in v1:
time: 649 us; the launch traced here: 647 us
  waiting for transfers between devices  286 us (44%)
  other arithmetic  165 us (25%)
  matrix products  99.2 us (15%)
  starting transfers between devices  61.5 us (9%)
  blocking collectives  14.5 us (2%)
  between operations  13.9 us (2%)
    ppermute x31, waiting for transfers between devices, passed_along(): return lax.ppermute(shard, axis, pairs)  285 us
    another operation x4, other arithmetic, block_terms(): lax.linalg.triangular_solve(lower, rhs_keys, left_side=True, lower=True,...  157 us
    ppermute x31, starting transfers between devices, passed_along(): return lax.ppermute(shard, axis, pairs)  61.4 us
    dot_general x47, matrix products, matmul_heads(): jnp.einsum('hef,hfg->heg', left, right, precision=lax.Precision.HIGHEST)  26 us
    dot_general x8, matrix products, advance(): jnp.einsum('...ce,...ef->...cf', decayed_query, state, precision=highest)  15.4 us
    all_to_all x1, blocking collectives, on_device(): got = lax.all_to_all(jnp.stack(shards), 'head', 0, 0)  14.5 us
  transfers between devices with their start and end apart: 32, of which 31 were waited for; matrix products, arithmetic and copies ran while one was open for 40% of the time, Pallas kernels for 0%

profile of v1, /device:TPU:24, one launch (start us, length us, event | category | flops | bytes accessed | tf_op | source)
XLA Modules:
  0.0 647.2 jit_solution(7920997251120607512)
XLA Ops:
  14.5 157.3 %custom-call.5 = f32[8,4,1,64,64]{3,4,2,1,0:T(8,128)S(1)} custom-call(f32[8,4,1,64,64]{4,3,2,1,0:T(8,128)S(1)} %fusion.30), custom_call_target="InvertDiagBlocksLowerTriangular" | custom-call | tf_op jit(solution)/shard_map/triangular_solve/custom-call.1 | solution.py:42
  178.3 2.1 fusion.35
  180.4 2.8 convolution_multiply_fusion
  183.2 4.9 fusion.42
  188.1 4.0 multiply_subtract_fusion
  192.1 14.6 %while.37 = (s32[]{:T(128)}, f32[4,128,128]{2,1,0:T(8,128)S(1)}, f32[4,128,128]{2,1,0:T(8,128)S(1)}, f32[8,4,128,128]{3,2,1,0:T(8,128)S(1)}, f32[8,4,128,128]{3,2,1,0:T(8,128)}, /*index=5*/s32[]{:T(128)}, s32[]{:T(128)}) while((s32[]{:T(128)}, f32[4,128,128]{2,1,0:T(8,128)S(1)}, f32[4,128,128]{2,1,0:T(8,128)S(1)}, ...), condition=%wide.region_3.5_spmd.clone, body=%wide.region_2.0_spmd.clone.sunk | while | flops 201457664 | bytes 2884699 | solution.py:104
  206.7 359.4 %while.35 = (s32[]{:T(128)}, f32[4,128,128]{2,1,0:T(8,128)S(1)}, f32[4,128,128]{2,1,0:T(8,128)S(1)}, f32[4,128,128]{2,1,0:T(8,128)S(1)}, s32[]{:T(128)}) while((s32[]{:T(128)}, f32[4,128,128]{2,1,0:T(8,128)S(1)}, f32[4,128,128]{2,1,0:T(8,128)S(1)}, f32[4,128,128]{2,1,0:T(8,128)S(1)}, s32[]{:T(128)}) %tuple.68), condition=%wide.region_5.7_spmd, body=%wide.region_4.6_spmd.sunk | while | flops 100728832 | bytes 2097253 | solution.py:110
  207.1 3.8 collective-permute-start
  211.0 10.4 %collective-permute-done = f32[4,128,128]{2,1,0:T(8,128)S(1)} collective-permute-done((f32[4,128,128]{2,1,0:T(8,128)S(1)}, f32[4,128,128]{2,1,0:T(8,128)S(1)}, u32[]{:S(2)}, u32[]{:S(2)}) %collective-permute-start) | collective-permute-done | bytes 262176 | tf_op jit(solution)/shard_map/while/body/eval_jaxpr/ppermute | solution.py:14
  223.7 9.6 %collective-permute-done = f32[4,128,128]{2,1,0:T(8,128)S(1)} collective-permute-done((f32[4,128,128]{2,1,0:T(8,128)S(1)}, f32[4,128,128]{2,1,0:T(8,128)S(1)}, u32[]{:S(2)}, u32[]{:S(2)}) %collective-permute-start) | collective-permute-done | bytes 262176 | tf_op jit(solution)/shard_map/while/body/eval_jaxpr/ppermute | solution.py:14
  235.6 8.6 %collective-permute-done = f32[4,128,128]{2,1,0:T(8,128)S(1)} collective-permute-done((f32[4,128,128]{2,1,0:T(8,128)S(1)}, f32[4,128,128]{2,1,0:T(8,128)S(1)}, u32[]{:S(2)}, u32[]{:S(2)}) %collective-permute-start) | collective-permute-done | bytes 262176 | tf_op jit(solution)/shard_map/while/body/eval_jaxpr/ppermute | solution.py:14
  246.6 8.4 %collective-permute-done = f32[4,128,128]{2,1,0:T(8,128)S(1)} collective-permute-done((f32[4,128,128]{2,1,0:T(8,128)S(1)}, f32[4,128,128]{2,1,0:T(8,128)S(1)}, u32[]{:S(2)}, u32[]{:S(2)}) %collective-permute-start) | collective-permute-done | bytes 262176 | tf_op jit(solution)/shard_map/while/body/eval_jaxpr/ppermute | solution.py:14
  257.3 8.4 %collective-permute-done = f32[4,128,128]{2,1,0:T(8,128)S(1)} collective-permute-done((f32[4,128,128]{2,1,0:T(8,128)S(1)}, f32[4,128,128]{2,1,0:T(8,128)S(1)}, u32[]{:S(2)}, u32[]{:S(2)}) %collective-permute-start) | collective-permute-done | bytes 262176 | tf_op jit(solution)/shard_map/while/body/eval_jaxpr/ppermute | solution.py:14
  268.1 8.4 %collective-permute-done = f32[4,128,128]{2,1,0:T(8,128)S(1)} collective-permute-done((f32[4,128,128]{2,1,0:T(8,128)S(1)}, f32[4,128,128]{2,1,0:T(8,128)S(1)}, u32[]{:S(2)}, u32[]{:S(2)}) %collective-permute-start) | collective-permute-done | bytes 262176 | tf_op jit(solution)/shard_map/while/body/eval_jaxpr/ppermute | solution.py:14
  278.9 8.5 %collective-permute-done = f32[4,128,128]{2,1,0:T(8,128)S(1)} collective-permute-done((f32[4,128,128]{2,1,0:T(8,128)S(1)}, f32[4,128,128]{2,1,0:T(8,128)S(1)}, u32[]{:S(2)}, u32[]{:S(2)}) %collective-permute-start) | collective-permute-done | bytes 262176 | tf_op jit(solution)/shard_map/while/body/eval_jaxpr/ppermute | solution.py:14
  287.8 1.9 collective-permute-start
  289.8 9.6 %collective-permute-done = f32[4,128,128]{2,1,0:T(8,128)S(1)} collective-permute-done((f32[4,128,128]{2,1,0:T(8,128)S(1)}, f32[4,128,128]{2,1,0:T(8,128)S(1)}, u32[]{:S(2)}, u32[]{:S(2)}) %collective-permute-start) | collective-permute-done | bytes 262176 | tf_op jit(solution)/shard_map/while/body/eval_jaxpr/ppermute | solution.py:14
  301.7 10.8 %collective-permute-done = f32[4,128,128]{2,1,0:T(8,128)S(1)} collective-permute-done((f32[4,128,128]{2,1,0:T(8,128)S(1)}, f32[4,128,128]{2,1,0:T(8,128)S(1)}, u32[]{:S(2)}, u32[]{:S(2)}) %collective-permute-start) | collective-permute-done | bytes 262176 | tf_op jit(solution)/shard_map/while/body/eval_jaxpr/ppermute | solution.py:14
  314.9 10.5 %collective-permute-done = f32[4,128,128]{2,1,0:T(8,128)S(1)} collective-permute-done((f32[4,128,128]{2,1,0:T(8,128)S(1)}, f32[4,128,128]{2,1,0:T(8,128)S(1)}, u32[]{:S(2)}, u32[]{:S(2)}) %collective-permute-start) | collective-permute-done | bytes 262176 | tf_op jit(solution)/shard_map/while/body/eval_jaxpr/ppermute | solution.py:14
  327.7 9.7 %collective-permute-done = f32[4,128,128]{2,1,0:T(8,128)S(1)} collective-permute-done((f32[4,128,128]{2,1,0:T(8,128)S(1)}, f32[4,128,128]{2,1,0:T(8,128)S(1)}, u32[]{:S(2)}, u32[]{:S(2)}) %collective-permute-start) | collective-permute-done | bytes 262176 | tf_op jit(solution)/shard_map/while/body/eval_jaxpr/ppermute | solution.py:14
  339.8 8.8 %collective-permute-done = f32[4,128,128]{2,1,0:T(8,128)S(1)} collective-permute-done((f32[4,128,128]{2,1,0:T(8,128)S(1)}, f32[4,128,128]{2,1,0:T(8,128)S(1)}, u32[]{:S(2)}, u32[]{:S(2)}) %collective-permute-start) | collective-permute-done | bytes 262176 | tf_op jit(solution)/shard_map/while/body/eval_jaxpr/ppermute | solution.py:14
  350.9 8.4 %collective-permute-done = f32[4,128,128]{2,1,0:T(8,128)S(1)} collective-permute-done((f32[4,128,128]{2,1,0:T(8,128)S(1)}, f32[4,128,128]{2,1,0:T(8,128)S(1)}, u32[]{:S(2)}, u32[]{:S(2)}) %collective-permute-start) | collective-permute-done | bytes 262176 | tf_op jit(solution)/shard_map/while/body/eval_jaxpr/ppermute | solution.py:14
  361.6 8.4 %collective-permute-done = f32[4,128,128]{2,1,0:T(8,128)S(1)} collective-permute-done((f32[4,128,128]{2,1,0:T(8,128)S(1)}, f32[4,128,128]{2,1,0:T(8,128)S(1)}, u32[]{:S(2)}, u32[]{:S(2)}) %collective-permute-start) | collective-permute-done | bytes 262176 | tf_op jit(solution)/shard_map/while/body/eval_jaxpr/ppermute | solution.py:14
  372.4 8.4 %collective-permute-done = f32[4,128,128]{2,1,0:T(8,128)S(1)} collective-permute-done((f32[4,128,128]{2,1,0:T(8,128)S(1)}, f32[4,128,128]{2,1,0:T(8,128)S(1)}, u32[]{:S(2)}, u32[]{:S(2)}) %collective-permute-start) | collective-permute-done | bytes 262176 | tf_op jit(solution)/shard_map/while/body/eval_jaxpr/ppermute | solution.py:14
  383.2 8.4 %collective-permute-done = f32[4,128,128]{2,1,0:T(8,128)S(1)} collective-permute-done((f32[4,128,128]{2,1,0:T(8,128)S(1)}, f32[4,128,128]{2,1,0:T(8,128)S(1)}, u32[]{:S(2)}, u32[]{:S(2)}) %collective-permute-start) | collective-permute-done | bytes 262176 | tf_op jit(solution)/shard_map/while/body/eval_jaxpr/ppermute | solution.py:14
  394.0 9.5 %collective-permute-done = f32[4,128,128]{2,1,0:T(8,128)S(1)} collective-permute-done((f32[4,128,128]{2,1,0:T(8,128)S(1)}, f32[4,128,128]{2,1,0:T(8,128)S(1)}, u32[]{:S(2)}, u32[]{:S(2)}) %collective-permute-start) | collective-permute-done | bytes 262176 | tf_op jit(solution)/shard_map/while/body/eval_jaxpr/ppermute | solution.py:14
  405.8 10.7 %collective-permute-done = f32[4,128,128]{2,1,0:T(8,128)S(1)} collective-permute-done((f32[4,128,128]{2,1,0:T(8,128)S(1)}, f32[4,128,128]{2,1,0:T(8,128)S(1)}, u32[]{:S(2)}, u32[]{:S(2)}) %collective-permute-start) | collective-permute-done | bytes 262176 | tf_op jit(solution)/shard_map/while/body/eval_jaxpr/ppermute | solution.py:14
  418.9 10.6 %collective-permute-done = f32[4,128,128]{2,1,0:T(8,128)S(1)} collective-permute-done((f32[4,128,128]{2,1,0:T(8,128)S(1)}, f32[4,128,128]{2,1,0:T(8,128)S(1)}, u32[]{:S(2)}, u32[]{:S(2)}) %collective-permute-start) | collective-permute-done | bytes 262176 | tf_op jit(solution)/shard_map/while/body/eval_jaxpr/ppermute | solution.py:14
  431.8 9.8 %collective-permute-done = f32[4,128,128]{2,1,0:T(8,128)S(1)} collective-permute-done((f32[4,128,128]{2,1,0:T(8,128)S(1)}, f32[4,128,128]{2,1,0:T(8,128)S(1)}, u32[]{:S(2)}, u32[]{:S(2)}) %collective-permute-start) | collective-permute-done | bytes 262176 | tf_op jit(solution)/shard_map/while/body/eval_jaxpr/ppermute | solution.py:14
  444.0 8.9 %collective-permute-done = f32[4,128,128]{2,1,0:T(8,128)S(1)} collective-permute-done((f32[4,128,128]{2,1,0:T(8,128)S(1)}, f32[4,128,128]{2,1,0:T(8,128)S(1)}, u32[]{:S(2)}, u32[]{:S(2)}) %collective-permute-start) | collective-permute-done | bytes 262176 | tf_op jit(solution)/shard_map/while/body/eval_jaxpr/ppermute | solution.py:14
  455.2 8.4 %collective-permute-done = f32[4,128,128]{2,1,0:T(8,128)S(1)} collective-permute-done((f32[4,128,128]{2,1,0:T(8,128)S(1)}, f32[4,128,128]{2,1,0:T(8,128)S(1)}, u32[]{:S(2)}, u32[]{:S(2)}) %collective-permute-start) | collective-permute-done | bytes 262176 | tf_op jit(solution)/shard_map/while/body/eval_jaxpr/ppermute | solution.py:14
  466.0 8.4 %collective-permute-done = f32[4,128,128]{2,1,0:T(8,128)S(1)} collective-permute-done((f32[4,128,128]{2,1,0:T(8,128)S(1)}, f32[4,128,128]{2,1,0:T(8,128)S(1)}, u32[]{:S(2)}, u32[]{:S(2)}) %collective-permute-start) | collective-permute-done | bytes 262176 | tf_op jit(solution)/shard_map/while/body/eval_jaxpr/ppermute | solution.py:14
  476.8 8.4 %collective-permute-done = f32[4,128,128]{2,1,0:T(8,128)S(1)} collective-permute-done((f32[4,128,128]{2,1,0:T(8,128)S(1)}, f32[4,128,128]{2,1,0:T(8,128)S(1)}, u32[]{:S(2)}, u32[]{:S(2)}) %collective-permute-start) | collective-permute-done | bytes 262176 | tf_op jit(solution)/shard_map/while/body/eval_jaxpr/ppermute | solution.py:14
  487.6 8.4 %collective-permute-done = f32[4,128,128]{2,1,0:T(8,128)S(1)} collective-permute-done((f32[4,128,128]{2,1,0:T(8,128)S(1)}, f32[4,128,128]{2,1,0:T(8,128)S(1)}, u32[]{:S(2)}, u32[]{:S(2)}) %collective-permute-start) | collective-permute-done | bytes 262176 | tf_op jit(solution)/shard_map/while/body/eval_jaxpr/ppermute | solution.py:14
  498.3 9.4 %collective-permute-done = f32[4,128,128]{2,1,0:T(8,128)S(1)} collective-permute-done((f32[4,128,128]{2,1,0:T(8,128)S(1)}, f32[4,128,128]{2,1,0:T(8,128)S(1)}, u32[]{:S(2)}, u32[]{:S(2)}) %collective-permute-start) | collective-permute-done | bytes 262176 | tf_op jit(solution)/shard_map/while/body/eval_jaxpr/ppermute | solution.py:14
  510.1 10.6 %collective-permute-done = f32[4,128,128]{2,1,0:T(8,128)S(1)} collective-permute-done((f32[4,128,128]{2,1,0:T(8,128)S(1)}, f32[4,128,128]{2,1,0:T(8,128)S(1)}, u32[]{:S(2)}, u32[]{:S(2)}) %collective-permute-start) | collective-permute-done | bytes 262176 | tf_op jit(solution)/shard_map/while/body/eval_jaxpr/ppermute | solution.py:14
  523.0 10.7 %collective-permute-done = f32[4,128,128]{2,1,0:T(8,128)S(1)} collective-permute-done((f32[4,128,128]{2,1,0:T(8,128)S(1)}, f32[4,128,128]{2,1,0:T(8,128)S(1)}, u32[]{:S(2)}, u32[]{:S(2)}) %collective-permute-start) | collective-permute-done | bytes 262176 | tf_op jit(solution)/shard_map/while/body/eval_jaxpr/ppermute | solution.py:14
  536.1 8.4 %collective-permute-done = f32[4,128,128]{2,1,0:T(8,128)S(1)} collective-permute-done((f32[4,128,128]{2,1,0:T(8,128)S(1)}, f32[4,128,128]{2,1,0:T(8,128)S(1)}, u32[]{:S(2)}, u32[]{:S(2)}) %collective-permute-start) | collective-permute-done | bytes 262176 | tf_op jit(solution)/shard_map/while/body/eval_jaxpr/ppermute | solution.py:14
  546.9 8.4 %collective-permute-done = f32[4,128,128]{2,1,0:T(8,128)S(1)} collective-permute-done((f32[4,128,128]{2,1,0:T(8,128)S(1)}, f32[4,128,128]{2,1,0:T(8,128)S(1)}, u32[]{:S(2)}, u32[]{:S(2)}) %collective-permute-start) | collective-permute-done | bytes 262176 | tf_op jit(solution)/shard_map/while/body/eval_jaxpr/ppermute | solution.py:14
  557.7 8.4 %collective-permute-done = f32[4,128,128]{2,1,0:T(8,128)S(1)} collective-permute-done((f32[4,128,128]{2,1,0:T(8,128)S(1)}, f32[4,128,128]{2,1,0:T(8,128)S(1)}, u32[]{:S(2)}, u32[]{:S(2)}) %collective-permute-start) | collective-permute-done | bytes 262176 | tf_op jit(solution)/shard_map/while/body/eval_jaxpr/ppermute | solution.py:14
  566.1 46.7 %while.36 = (s32[]{:T(128)}, f32[4,128,128]{2,1,0:T(8,128)S(1)}, f32[8,4,64,128]{3,2,0,1:T(8,128)}, f32[8,4,128,128]{3,2,1,0:T(8,128)S(1)}, f32[8,4,128,128]{3,2...) while((s32[]{:T(128)}, f32[4,128,128]{2,1,0:T(8,128)S(1)}, ...), condition=%wide.region_8.10_spmd, body=%wide.region_7.9_spmd.sunk | while | flops 226623488 | bytes 3280485 | solution.py:65
  568.7 1.9 fusion.93
  574.5 1.9 fusion.93
  580.4 1.9 fusion.93
  586.2 1.9 fusion.93
  609.5 1.9 fusion.93
  616.3 14.5 %all_to_all.5 = bf16[8,64,512]{2,1,0:T(8,128)(2,1)S(1)} all-to-all(bf16[8,64,512]{2,1,0:T(8,128)(2,1)S(1)} %constant_dynamic-update-slice_fusion), channel_id=1, replica_groups=mesh['seq'=32,'head'=8] {'head'}, dimensions={0} | all-to-all | bytes 1048576 | tf_op jit(solution)/shard_map/all_to_all | solution.py:119
  630.9 9.5 %convolution_convert_fusion = bf16[64,2048]{1,0:T(8,128)(2,1)} fusion(bf16[64,4096]{1,0:T(8,128)(2,1)S(1)} %bitcast.128, bf16[4096,2048]{1,0:T(8,128)(2,1)} %all-gather.2.cloned.1.call-done), kind=kOutput, calls=%fused_computation.31 | convolution fusion | flops 1073872896 | bytes 17563648 | tf_op jit(solution)/shard_map/dot_general | solution.py:121
  (219 shorter events, 136.5 us)
Async XLA Ops:
  6.5 0.8 copy-start.9
  6.5 0.8 copy-start.6
  6.5 0.9 copy-start.7
  6.5 1.0 copy-start.4
  6.5 624.3 %all-gather.2.cloned.1.call-start = ((), (), s32[]{:S(2)}) async-start(), calls=%async_computation.1 | async-start | bytes 18874368 | tf_op jit(solution)/shard_map/all_gather | solution.py:123
  7.6 1.6 copy-start.5
  178.3 9.8 %copy-start = (f32[8,4,64,128]{3,2,1,0:T(8,128)}, f32[8,4,64,128]{3,2,1,0:T(8,128)S(1)}, u32[]{:S(2)}) copy-start(f32[8,4,64,128]{3,2,1,0:T(8,128)S(1)} %fusion.37) | copy-start | bytes 3145732
  180.4 7.7 %copy-start.1 = (f32[8,4,64,128]{3,2,1,0:T(8,128)}, f32[8,4,64,128]{3,2,1,0:T(8,128)S(1)}, u32[]{:S(2)}) copy-start(f32[8,4,64,128]{3,2,1,0:T(8,128)S(1)} %fusion.35) | copy-start | bytes 3145732
  207.1 14.2 %collective-permute-start = (f32[4,128,128]{2,1,0:T(8,128)S(1)}, f32[4,128,128]{2,1,0:T(8,128)S(1)}, u32[]{:S(2)}, u32[]{:S(2)}) collective-permute-start(f32[4,128,128]{2,1,0:T(8,128)S(1)} %convolution_add_fusion.7), channel_id=1, source_target_pairs={{0,8},{8,16},{16,24},{24,32},{32,40},{40,48},{48,56},{56,64},{64,7... | collective-permute-start | bytes 786440 | tf_op jit(solution)/shard_map/while/body/eval_jaxpr/ppermute | solution.py:14
  221.8 11.5 %collective-permute-start = (f32[4,128,128]{2,1,0:T(8,128)S(1)}, f32[4,128,128]{2,1,0:T(8,128)S(1)}, u32[]{:S(2)}, u32[]{:S(2)}) collective-permute-start(f32[4,128,128]{2,1,0:T(8,128)S(1)} %convolution_add_fusion.7), channel_id=1, source_target_pairs={{0,8},{8,16},{16,24},{24,32},{32,40},{40,48},{48,56},{56,64},{64,7... | collective-permute-start | bytes 786440 | tf_op jit(solution)/shard_map/while/body/eval_jaxpr/ppermute | solution.py:14
  233.7 10.6 %collective-permute-start = (f32[4,128,128]{2,1,0:T(8,128)S(1)}, f32[4,128,128]{2,1,0:T(8,128)S(1)}, u32[]{:S(2)}, u32[]{:S(2)}) collective-permute-start(f32[4,128,128]{2,1,0:T(8,128)S(1)} %convolution_add_fusion.7), channel_id=1, source_target_pairs={{0,8},{8,16},{16,24},{24,32},{32,40},{40,48},{48,56},{56,64},{64,7... | collective-permute-start | bytes 786440 | tf_op jit(solution)/shard_map/while/body/eval_jaxpr/ppermute | solution.py:14
  244.6 10.4 %collective-permute-start = (f32[4,128,128]{2,1,0:T(8,128)S(1)}, f32[4,128,128]{2,1,0:T(8,128)S(1)}, u32[]{:S(2)}, u32[]{:S(2)}) collective-permute-start(f32[4,128,128]{2,1,0:T(8,128)S(1)} %convolution_add_fusion.7), channel_id=1, source_target_pairs={{0,8},{8,16},{16,24},{24,32},{32,40},{40,48},{48,56},{56,64},{64,7... | collective-permute-start | bytes 786440 | tf_op jit(solution)/shard_map/while/body/eval_jaxpr/ppermute | solution.py:14
  255.4 10.4 %collective-permute-start = (f32[4,128,128]{2,1,0:T(8,128)S(1)}, f32[4,128,128]{2,1,0:T(8,128)S(1)}, u32[]{:S(2)}, u32[]{:S(2)}) collective-permute-start(f32[4,128,128]{2,1,0:T(8,128)S(1)} %convolution_add_fusion.7), channel_id=1, source_target_pairs={{0,8},{8,16},{16,24},{24,32},{32,40},{40,48},{48,56},{56,64},{64,7... | collective-permute-start | bytes 786440 | tf_op jit(solution)/shard_map/while/body/eval_jaxpr/ppermute | solution.py:14
  266.2 10.4 %collective-permute-start = (f32[4,128,128]{2,1,0:T(8,128)S(1)}, f32[4,128,128]{2,1,0:T(8,128)S(1)}, u32[]{:S(2)}, u32[]{:S(2)}) collective-permute-start(f32[4,128,128]{2,1,0:T(8,128)S(1)} %convolution_add_fusion.7), channel_id=1, source_target_pairs={{0,8},{8,16},{16,24},{24,32},{32,40},{40,48},{48,56},{56,64},{64,7... | collective-permute-start | bytes 786440 | tf_op jit(solution)/shard_map/while/body/eval_jaxpr/ppermute | solution.py:14
  277.0 10.5 %collective-permute-start = (f32[4,128,128]{2,1,0:T(8,128)S(1)}, f32[4,128,128]{2,1,0:T(8,128)S(1)}, u32[]{:S(2)}, u32[]{:S(2)}) collective-permute-start(f32[4,128,128]{2,1,0:T(8,128)S(1)} %convolution_add_fusion.7), channel_id=1, source_target_pairs={{0,8},{8,16},{16,24},{24,32},{32,40},{40,48},{48,56},{56,64},{64,7... | collective-permute-start | bytes 786440 | tf_op jit(solution)/shard_map/while/body/eval_jaxpr/ppermute | solution.py:14
  287.8 11.5 %collective-permute-start = (f32[4,128,128]{2,1,0:T(8,128)S(1)}, f32[4,128,128]{2,1,0:T(8,128)S(1)}, u32[]{:S(2)}, u32[]{:S(2)}) collective-permute-start(f32[4,128,128]{2,1,0:T(8,128)S(1)} %convolution_add_fusion.7), channel_id=1, source_target_pairs={{0,8},{8,16},{16,24},{24,32},{32,40},{40,48},{48,56},{56,64},{64,7... | collective-permute-start | bytes 786440 | tf_op jit(solution)/shard_map/while/body/eval_jaxpr/ppermute | solution.py:14
  299.8 12.8 %collective-permute-start = (f32[4,128,128]{2,1,0:T(8,128)S(1)}, f32[4,128,128]{2,1,0:T(8,128)S(1)}, u32[]{:S(2)}, u32[]{:S(2)}) collective-permute-start(f32[4,128,128]{2,1,0:T(8,128)S(1)} %convolution_add_fusion.7), channel_id=1, source_target_pairs={{0,8},{8,16},{16,24},{24,32},{32,40},{40,48},{48,56},{56,64},{64,7... | collective-permute-start | bytes 786440 | tf_op jit(solution)/shard_map/while/body/eval_jaxpr/ppermute | solution.py:14
  313.0 12.4 %collective-permute-start = (f32[4,128,128]{2,1,0:T(8,128)S(1)}, f32[4,128,128]{2,1,0:T(8,128)S(1)}, u32[]{:S(2)}, u32[]{:S(2)}) collective-permute-start(f32[4,128,128]{2,1,0:T(8,128)S(1)} %convolution_add_fusion.7), channel_id=1, source_target_pairs={{0,8},{8,16},{16,24},{24,32},{32,40},{40,48},{48,56},{56,64},{64,7... | collective-permute-start | bytes 786440 | tf_op jit(solution)/shard_map/while/body/eval_jaxpr/ppermute | solution.py:14
  325.8 11.6 %collective-permute-start = (f32[4,128,128]{2,1,0:T(8,128)S(1)}, f32[4,128,128]{2,1,0:T(8,128)S(1)}, u32[]{:S(2)}, u32[]{:S(2)}) collective-permute-start(f32[4,128,128]{2,1,0:T(8,128)S(1)} %convolution_add_fusion.7), channel_id=1, source_target_pairs={{0,8},{8,16},{16,24},{24,32},{32,40},{40,48},{48,56},{56,64},{64,7... | collective-permute-start | bytes 786440 | tf_op jit(solution)/shard_map/while/body/eval_jaxpr/ppermute | solution.py:14
  337.8 10.7 %collective-permute-start = (f32[4,128,128]{2,1,0:T(8,128)S(1)}, f32[4,128,128]{2,1,0:T(8,128)S(1)}, u32[]{:S(2)}, u32[]{:S(2)}) collective-permute-start(f32[4,128,128]{2,1,0:T(8,128)S(1)} %convolution_add_fusion.7), channel_id=1, source_target_pairs={{0,8},{8,16},{16,24},{24,32},{32,40},{40,48},{48,56},{56,64},{64,7... | collective-permute-start | bytes 786440 | tf_op jit(solution)/shard_map/while/body/eval_jaxpr/ppermute | solution.py:14
  348.9 10.4 %collective-permute-start = (f32[4,128,128]{2,1,0:T(8,128)S(1)}, f32[4,128,128]{2,1,0:T(8,128)S(1)}, u32[]{:S(2)}, u32[]{:S(2)}) collective-permute-start(f32[4,128,128]{2,1,0:T(8,128)S(1)} %convolution_add_fusion.7), channel_id=1, source_target_pairs={{0,8},{8,16},{16,24},{24,32},{32,40},{40,48},{48,56},{56,64},{64,7... | collective-permute-start | bytes 786440 | tf_op jit(solution)/shard_map/while/body/eval_jaxpr/ppermute | solution.py:14
  359.7 10.4 %collective-permute-start = (f32[4,128,128]{2,1,0:T(8,128)S(1)}, f32[4,128,128]{2,1,0:T(8,128)S(1)}, u32[]{:S(2)}, u32[]{:S(2)}) collective-permute-start(f32[4,128,128]{2,1,0:T(8,128)S(1)} %convolution_add_fusion.7), channel_id=1, source_target_pairs={{0,8},{8,16},{16,24},{24,32},{32,40},{40,48},{48,56},{56,64},{64,7... | collective-permute-start | bytes 786440 | tf_op jit(solution)/shard_map/while/body/eval_jaxpr/ppermute | solution.py:14
  370.5 10.4 %collective-permute-start = (f32[4,128,128]{2,1,0:T(8,128)S(1)}, f32[4,128,128]{2,1,0:T(8,128)S(1)}, u32[]{:S(2)}, u32[]{:S(2)}) collective-permute-start(f32[4,128,128]{2,1,0:T(8,128)S(1)} %convolution_add_fusion.7), channel_id=1, source_target_pairs={{0,8},{8,16},{16,24},{24,32},{32,40},{40,48},{48,56},{56,64},{64,7... | collective-permute-start | bytes 786440 | tf_op jit(solution)/shard_map/while/body/eval_jaxpr/ppermute | solution.py:14
  381.3 10.4 %collective-permute-start = (f32[4,128,128]{2,1,0:T(8,128)S(1)}, f32[4,128,128]{2,1,0:T(8,128)S(1)}, u32[]{:S(2)}, u32[]{:S(2)}) collective-permute-start(f32[4,128,128]{2,1,0:T(8,128)S(1)} %convolution_add_fusion.7), channel_id=1, source_target_pairs={{0,8},{8,16},{16,24},{24,32},{32,40},{40,48},{48,56},{56,64},{64,7... | collective-permute-start | bytes 786440 | tf_op jit(solution)/shard_map/while/body/eval_jaxpr/ppermute | solution.py:14
  392.0 11.5 %collective-permute-start = (f32[4,128,128]{2,1,0:T(8,128)S(1)}, f32[4,128,128]{2,1,0:T(8,128)S(1)}, u32[]{:S(2)}, u32[]{:S(2)}) collective-permute-start(f32[4,128,128]{2,1,0:T(8,128)S(1)} %convolution_add_fusion.7), channel_id=1, source_target_pairs={{0,8},{8,16},{16,24},{24,32},{32,40},{40,48},{48,56},{56,64},{64,7... | collective-permute-start | bytes 786440 | tf_op jit(solution)/shard_map/while/body/eval_jaxpr/ppermute | solution.py:14
  403.9 12.7 %collective-permute-start = (f32[4,128,128]{2,1,0:T(8,128)S(1)}, f32[4,128,128]{2,1,0:T(8,128)S(1)}, u32[]{:S(2)}, u32[]{:S(2)}) collective-permute-start(f32[4,128,128]{2,1,0:T(8,128)S(1)} %convolution_add_fusion.7), channel_id=1, source_target_pairs={{0,8},{8,16},{16,24},{24,32},{32,40},{40,48},{48,56},{56,64},{64,7... | collective-permute-start | bytes 786440 | tf_op jit(solution)/shard_map/while/body/eval_jaxpr/ppermute | solution.py:14
  417.0 12.6 %collective-permute-start = (f32[4,128,128]{2,1,0:T(8,128)S(1)}, f32[4,128,128]{2,1,0:T(8,128)S(1)}, u32[]{:S(2)}, u32[]{:S(2)}) collective-permute-start(f32[4,128,128]{2,1,0:T(8,128)S(1)} %convolution_add_fusion.7), channel_id=1, source_target_pairs={{0,8},{8,16},{16,24},{24,32},{32,40},{40,48},{48,56},{56,64},{64,7... | collective-permute-start | bytes 786440 | tf_op jit(solution)/shard_map/while/body/eval_jaxpr/ppermute | solution.py:14
  429.9 11.8 %collective-permute-start = (f32[4,128,128]{2,1,0:T(8,128)S(1)}, f32[4,128,128]{2,1,0:T(8,128)S(1)}, u32[]{:S(2)}, u32[]{:S(2)}) collective-permute-start(f32[4,128,128]{2,1,0:T(8,128)S(1)} %convolution_add_fusion.7), channel_id=1, source_target_pairs={{0,8},{8,16},{16,24},{24,32},{32,40},{40,48},{48,56},{56,64},{64,7... | collective-permute-start | bytes 786440 | tf_op jit(solution)/shard_map/while/body/eval_jaxpr/ppermute | solution.py:14
  442.1 10.8 %collective-permute-start = (f32[4,128,128]{2,1,0:T(8,128)S(1)}, f32[4,128,128]{2,1,0:T(8,128)S(1)}, u32[]{:S(2)}, u32[]{:S(2)}) collective-permute-start(f32[4,128,128]{2,1,0:T(8,128)S(1)} %convolution_add_fusion.7), channel_id=1, source_target_pairs={{0,8},{8,16},{16,24},{24,32},{32,40},{40,48},{48,56},{56,64},{64,7... | collective-permute-start | bytes 786440 | tf_op jit(solution)/shard_map/while/body/eval_jaxpr/ppermute | solution.py:14
  453.3 10.4 %collective-permute-start = (f32[4,128,128]{2,1,0:T(8,128)S(1)}, f32[4,128,128]{2,1,0:T(8,128)S(1)}, u32[]{:S(2)}, u32[]{:S(2)}) collective-permute-start(f32[4,128,128]{2,1,0:T(8,128)S(1)} %convolution_add_fusion.7), channel_id=1, source_target_pairs={{0,8},{8,16},{16,24},{24,32},{32,40},{40,48},{48,56},{56,64},{64,7... | collective-permute-start | bytes 786440 | tf_op jit(solution)/shard_map/while/body/eval_jaxpr/ppermute | solution.py:14
  464.1 10.4 %collective-permute-start = (f32[4,128,128]{2,1,0:T(8,128)S(1)}, f32[4,128,128]{2,1,0:T(8,128)S(1)}, u32[]{:S(2)}, u32[]{:S(2)}) collective-permute-start(f32[4,128,128]{2,1,0:T(8,128)S(1)} %convolution_add_fusion.7), channel_id=1, source_target_pairs={{0,8},{8,16},{16,24},{24,32},{32,40},{40,48},{48,56},{56,64},{64,7... | collective-permute-start | bytes 786440 | tf_op jit(solution)/shard_map/while/body/eval_jaxpr/ppermute | solution.py:14
  474.9 10.4 %collective-permute-start = (f32[4,128,128]{2,1,0:T(8,128)S(1)}, f32[4,128,128]{2,1,0:T(8,128)S(1)}, u32[]{:S(2)}, u32[]{:S(2)}) collective-permute-start(f32[4,128,128]{2,1,0:T(8,128)S(1)} %convolution_add_fusion.7), channel_id=1, source_target_pairs={{0,8},{8,16},{16,24},{24,32},{32,40},{40,48},{48,56},{56,64},{64,7... | collective-permute-start | bytes 786440 | tf_op jit(solution)/shard_map/while/body/eval_jaxpr/ppermute | solution.py:14
  485.6 10.4 %collective-permute-start = (f32[4,128,128]{2,1,0:T(8,128)S(1)}, f32[4,128,128]{2,1,0:T(8,128)S(1)}, u32[]{:S(2)}, u32[]{:S(2)}) collective-permute-start(f32[4,128,128]{2,1,0:T(8,128)S(1)} %convolution_add_fusion.7), channel_id=1, source_target_pairs={{0,8},{8,16},{16,24},{24,32},{32,40},{40,48},{48,56},{56,64},{64,7... | collective-permute-start | bytes 786440 | tf_op jit(solution)/shard_map/while/body/eval_jaxpr/ppermute | solution.py:14
  496.4 11.4 %collective-permute-start = (f32[4,128,128]{2,1,0:T(8,128)S(1)}, f32[4,128,128]{2,1,0:T(8,128)S(1)}, u32[]{:S(2)}, u32[]{:S(2)}) collective-permute-start(f32[4,128,128]{2,1,0:T(8,128)S(1)} %convolution_add_fusion.7), channel_id=1, source_target_pairs={{0,8},{8,16},{16,24},{24,32},{32,40},{40,48},{48,56},{56,64},{64,7... | collective-permute-start | bytes 786440 | tf_op jit(solution)/shard_map/while/body/eval_jaxpr/ppermute | solution.py:14
  508.2 12.6 %collective-permute-start = (f32[4,128,128]{2,1,0:T(8,128)S(1)}, f32[4,128,128]{2,1,0:T(8,128)S(1)}, u32[]{:S(2)}, u32[]{:S(2)}) collective-permute-start(f32[4,128,128]{2,1,0:T(8,128)S(1)} %convolution_add_fusion.7), channel_id=1, source_target_pairs={{0,8},{8,16},{16,24},{24,32},{32,40},{40,48},{48,56},{56,64},{64,7... | collective-permute-start | bytes 786440 | tf_op jit(solution)/shard_map/while/body/eval_jaxpr/ppermute | solution.py:14
  521.1 12.7 %collective-permute-start = (f32[4,128,128]{2,1,0:T(8,128)S(1)}, f32[4,128,128]{2,1,0:T(8,128)S(1)}, u32[]{:S(2)}, u32[]{:S(2)}) collective-permute-start(f32[4,128,128]{2,1,0:T(8,128)S(1)} %convolution_add_fusion.7), channel_id=1, source_target_pairs={{0,8},{8,16},{16,24},{24,32},{32,40},{40,48},{48,56},{56,64},{64,7... | collective-permute-start | bytes 786440 | tf_op jit(solution)/shard_map/while/body/eval_jaxpr/ppermute | solution.py:14
  534.2 10.4 %collective-permute-start = (f32[4,128,128]{2,1,0:T(8,128)S(1)}, f32[4,128,128]{2,1,0:T(8,128)S(1)}, u32[]{:S(2)}, u32[]{:S(2)}) collective-permute-start(f32[4,128,128]{2,1,0:T(8,128)S(1)} %convolution_add_fusion.7), channel_id=1, source_target_pairs={{0,8},{8,16},{16,24},{24,32},{32,40},{40,48},{48,56},{56,64},{64,7... | collective-permute-start | bytes 786440 | tf_op jit(solution)/shard_map/while/body/eval_jaxpr/ppermute | solution.py:14
  545.0 10.4 %collective-permute-start = (f32[4,128,128]{2,1,0:T(8,128)S(1)}, f32[4,128,128]{2,1,0:T(8,128)S(1)}, u32[]{:S(2)}, u32[]{:S(2)}) collective-permute-start(f32[4,128,128]{2,1,0:T(8,128)S(1)} %convolution_add_fusion.7), channel_id=1, source_target_pairs={{0,8},{8,16},{16,24},{24,32},{32,40},{40,48},{48,56},{56,64},{64,7... | collective-permute-start | bytes 786440 | tf_op jit(solution)/shard_map/while/body/eval_jaxpr/ppermute | solution.py:14
  555.7 10.4 %collective-permute-start = (f32[4,128,128]{2,1,0:T(8,128)S(1)}, f32[4,128,128]{2,1,0:T(8,128)S(1)}, u32[]{:S(2)}, u32[]{:S(2)}) collective-permute-start(f32[4,128,128]{2,1,0:T(8,128)S(1)} %convolution_add_fusion.7), channel_id=1, source_target_pairs={{0,8},{8,16},{16,24},{24,32},{32,40},{40,48},{48,56},{56,64},{64,7... | collective-permute-start | bytes 786440 | tf_op jit(solution)/shard_map/while/body/eval_jaxpr/ppermute | solution.py:14
  566.1 48.5 %copy-start.3 = (bf16[512,512]{1,0:T(8,128)(2,1)S(1)}, bf16[512,512]{1,0:T(8,128)(2,1)}, u32[]{:S(2)}) copy-start(bf16[512,512]{1,0:T(8,128)(2,1)} %param.24) | copy-start | bytes 1572868
  612.8 2.2 copy-start.2
  612.8 2.2 copy-start.8
Sparse Core Ops, SparseCore 0:
  9.2 90.6 all-gather.1
